TPU v7x, 128 devices: a whole 4x4x4 slice. The times are simulated.
128 devices in a mesh: region: 16 (over y, z_hi, core), pos: 8 (over z_lo, x).
Axes of the slice: x: 4, y: 4, z: 4 (z_hi: 2, z_lo: 2; z = z_hi * 2 + z_lo), core: 2. Of those that a mesh axis runs over, the one named last changes fastest.
Arguments:
- object_tiles: float32 [256, 2, 2, 128, 128], P('region'), may hold values from -4 to 4
- probe: float32 [4, 2, 256, 256], replicated, may hold values from -3 to 3
- fresnel_phase: float32 [256, 256], replicated, may hold values from -3.140625 to 3.140625
- patterns: float32 [16, 8, 2, 256, 256], P('region', 'pos'), may hold values from 0 to 4
- row_offsets: int32 [16, 8, 2], P('region', 'pos'), may hold values from 0 to 3840, as said below
- col_offsets: int32 [16, 8, 2], P('region', 'pos'), may hold values from 0 to 768
- counts: int32 [16, 8], P('region', 'pos'), may hold values from 1 to 2, as said below
Outputs:
- new_object: float32 [256, 2, 2, 128, 128], P('region')
Inputs may be any that keep to these rules, and one draw needn't show every extreme that they name: A device's live positions are its first counts slots; the other slots of its position arrays are ignored. Some device holds 2 live positions. `row_offsets`: every slot of region index r starts at a row from r * 2 * 128 to r * 2 * 128 + 2 * 128 - 1, and never after row 3840.
All inputs are finite; a program needn't handle non-finite values.
Results may differ from a plain program's by a relative error of at most 0.0095.
Values sent between devices are 32-bit elements; how exact they have to be, the bound alone decides.
No kernel may reach another device: no remote copies, remote signals or barrier semaphores. Data moves between devices by JAX's collectives and lax.ppermute only.
A program may use at most 128 MiB of HBM per device.

v0:
```python
import math
import jax
import jax.numpy as jnp
from jax import lax
from jax.sharding import PartitionSpec as P

TGX = 8
step_size = 0.05


def shifted(shard, axis, by):
    count = lax.axis_size(axis)
    pairs = [(i, i + by) for i in range(count) if 0 <= i + by < count]
    return lax.ppermute(shard, axis, pairs)


def make_tables(length):
    counter = jnp.arange(length, dtype=jnp.int32)
    product = counter[:, None] * counter[None, :] % length
    angles = product.astype(jnp.float32) * jnp.float32(2.0 * math.pi / length)
    factor = jnp.float32(1.0 / math.sqrt(length))
    return (
        (jnp.cos(angles) * factor).astype(jnp.bfloat16),
        (jnp.sin(angles) * factor).astype(jnp.bfloat16),
    )


def left_product(matrix, field):
    return jnp.einsum("jk,mkl->mjl", matrix, field, preferred_element_type=jnp.float32)


def right_product(field, matrix):
    return jnp.einsum("mjk,kl->mjl", field, matrix, preferred_element_type=jnp.float32)


def transform(field_re, field_im, direction, cos_table, sin_table):
    upper_re = left_product(cos_table, field_re) - direction * left_product(sin_table, field_im)
    upper_im = left_product(cos_table, field_im) + direction * left_product(sin_table, field_re)
    upper_re = upper_re.astype(jnp.bfloat16)
    upper_im = upper_im.astype(jnp.bfloat16)
    result_re = right_product(upper_re, cos_table) - direction * right_product(upper_im, sin_table)
    result_im = right_product(upper_im, cos_table) + direction * right_product(upper_re, sin_table)
    return (result_re, result_im)


def complex_product(left_re, left_im, right_re, right_im):
    return (left_re * right_re - left_im * right_im, left_re * right_im + left_im * right_re)


def conj_product(left_re, left_im, right_re, right_im):
    return (left_re * right_re + left_im * right_im, left_re * right_im - left_im * right_re)


def position_gradient(patch, probe, wave_re, wave_im, measured, cos_table, sin_table):
    slice_count = patch.shape[0]
    field_re = probe[:, 0]
    field_im = probe[:, 1]
    incoming = []
    for layer_index in range(slice_count):
        incoming.append((field_re, field_im))
        exit_re, exit_im = complex_product(
            field_re, field_im, patch[layer_index, 0], patch[layer_index, 1]
        )
        exit_re = exit_re.astype(jnp.bfloat16)
        exit_im = exit_im.astype(jnp.bfloat16)
        if layer_index + 1 < slice_count:
            spec_re, spec_im = transform(exit_re, exit_im, -1.0, cos_table, sin_table)
            spec_re, spec_im = complex_product(wave_re, wave_im, spec_re, spec_im)
            field_re, field_im = transform(
                spec_re.astype(jnp.bfloat16),
                spec_im.astype(jnp.bfloat16),
                1.0,
                cos_table,
                sin_table,
            )
    far_re, far_im = transform(exit_re, exit_im, -1.0, cos_table, sin_table)
    intensity = jnp.sum(far_re * far_re + far_im * far_im, axis=0)
    misfit = intensity - measured
    back_re, back_im = transform(
        (misfit * far_re).astype(jnp.bfloat16),
        (misfit * far_im).astype(jnp.bfloat16),
        1.0,
        cos_table,
        sin_table,
    )
    results = [None] * slice_count
    for layer_index in reversed(range(slice_count)):
        incident_re, incident_im = incoming[layer_index]
        grad_re, grad_im = conj_product(incident_re, incident_im, back_re, back_im)
        results[layer_index] = jnp.stack([jnp.sum(grad_re, axis=0), jnp.sum(grad_im, axis=0)])
        if layer_index > 0:
            prior_re, prior_im = conj_product(
                patch[layer_index, 0], patch[layer_index, 1], back_re, back_im
            )
            spec_re, spec_im = transform(
                prior_re.astype(jnp.bfloat16),
                prior_im.astype(jnp.bfloat16),
                -1.0,
                cos_table,
                sin_table,
            )
            spec_re, spec_im = conj_product(wave_re, wave_im, spec_re, spec_im)
            back_re, back_im = transform(
                spec_re.astype(jnp.bfloat16),
                spec_im.astype(jnp.bfloat16),
                1.0,
                cos_table,
                sin_table,
            )
    return jnp.stack(results)


def tiles_to_band(tiles, band_tiles, tile_side):
    slice_count = tiles.shape[1]
    across = tiles.shape[0] // band_tiles
    shaped = tiles.reshape(band_tiles, across, slice_count, 2, tile_side, tile_side).transpose(
        2, 3, 0, 4, 1, 5
    )
    return shaped.reshape(slice_count, 2, band_tiles * tile_side, across * tile_side)


def per_device(object_tiles, probe, fresnel_phase, patterns, row_offsets, col_offsets, counts):
    slot_count = patterns.shape[2]
    pattern_side = patterns.shape[-1]
    tile_side = object_tiles.shape[-1]
    slice_count = object_tiles.shape[1]
    held_tiles = object_tiles.shape[0]
    band_tiles = held_tiles // TGX
    band_rows = band_tiles * tile_side
    width_pixels = TGX * tile_side
    measured = patterns.reshape(slot_count, pattern_side, pattern_side)
    row_start = row_offsets.reshape(slot_count)
    col_start = col_offsets.reshape(slot_count)
    live_count = counts.reshape(())
    following = shifted(object_tiles, "region", -1)
    canvas = jnp.concatenate(
        [
            tiles_to_band(object_tiles, band_tiles, tile_side),
            tiles_to_band(following, band_tiles, tile_side),
        ],
        axis=2,
    )
    band_first = lax.axis_index("region") * band_rows
    cos_table, sin_table = make_tables(pattern_side)
    wave_re = jnp.cos(fresnel_phase)
    wave_im = jnp.sin(fresnel_phase)
    zero_index = jnp.int32(0)

    def one_position(position, gradient):
        local_row = row_start[position] - band_first
        local_col = col_start[position]
        corner = (zero_index, zero_index, local_row, local_col)
        patch = lax.dynamic_slice(canvas, corner, (slice_count, 2, pattern_side, pattern_side))
        term = position_gradient(
            patch, probe, wave_re, wave_im, measured[position], cos_table, sin_table
        )
        former = lax.dynamic_slice(gradient, corner, (slice_count, 2, pattern_side, pattern_side))
        return lax.dynamic_update_slice(gradient, former + term, corner)

    empty = jnp.zeros((slice_count, 2, 2 * band_rows, width_pixels), jnp.float32)
    gradient = lax.fori_loop(0, live_count, one_position, empty)
    shaped = gradient.reshape(slice_count, 2, 2, band_tiles, tile_side, TGX, tile_side).transpose(
        2, 3, 5, 0, 1, 4, 6
    )
    shaped = shaped.reshape(2, held_tiles * slice_count * 2 * tile_side, tile_side)
    own_rows = shaped[0]
    spill_rows = shaped[1]
    held_rows = object_tiles.reshape(-1, tile_side)
    arrived = shifted(spill_rows, "region", 1)
    combined = lax.psum(own_rows + arrived, "pos")
    return (held_rows - step_size * combined).reshape(object_tiles.shape)


def solution(mesh):
    in_specs = (
        P("region", None, None, None, None),
        P(),
        P(),
        P("region", "pos", None, None, None),
        P("region", "pos", None),
        P("region", "pos", None),
        P("region", "pos"),
    )
    out_specs = P("region", None, None, None, None)
    return jax.shard_map(
        per_device, mesh=mesh, in_specs=in_specs, out_specs=out_specs, check_vma=False
    )
```

profile of v0, /device:TPU:1, one launch (start us, length us, event | category | flops | bytes accessed | tf_op | source)
XLA Modules:
  0.0 442.0 jit_solution(3993360952174075984)
XLA Ops:
  6.5 3.3 collective-permute-start
  9.8 1.9 copy.58
  12.7 4.4 copy.113
  17.0 4.9 %reshape.50 = f32[2,2,256,1024]{3,2,1,0:T(8,128)} reshape(f32[2,2,2,128,8,128]{5,4,3,2,1,0:T(8,128)} %bitcast.461) | data formatting | bytes 8388608 | tf_op jit(solution)/shard_map/reshape | solution.py:119
  22.0 1.6 fusion.370
  23.6 36.4 %collective-permute-done = f32[16,2,2,128,128]{4,3,2,1,0:T(8,128)} collective-permute-done((f32[16,2,2,128,128]{4,3,2,1,0:T(8,128)}, f32[16,2,2,128,128]{4,3,2,1,0:T(8,128)}, u32[]{:S(2)}, u32[]{:S(2)}) %collective-permute-start) | collective-permute-done | bytes 4194336 | tf_op jit(solution)/shard_map/ppermute | solution.py:14
  59.9 6.6 %copy.112 = f32[2,8,2,2,128,128]{5,1,4,0,3,2:T(8,128)} copy(f32[2,8,2,2,128,128]{5,4,3,2,1,0:T(8,128)} %bitcast.6) | data formatting | bytes 8388608 | tf_op jit(solution)/shard_map/reshape | solution.py:116
  66.5 4.9 %reshape.52 = f32[2,2,256,1024]{3,2,1,0:T(8,128)} reshape(f32[2,2,2,128,8,128]{5,4,3,2,1,0:T(8,128)} %bitcast.460) | data formatting | bytes 8388608 | tf_op jit(solution)/shard_map/reshape | solution.py:119
  71.4 8.3 %pad_maximum_fusion = f32[2,2,512,1024]{3,2,1,0:T(8,128)} fusion(f32[2,2,256,1024]{3,2,1,0:T(8,128)} %reshape.52, f32[2,2,256,1024]{3,2,1,0:T(8,128)} %reshape.50), kind=kLoop, calls=%fused_computation.377 | loop fusion | flops 2097152 | bytes 16777216 | tf_op jit(solution)/shard_map/concatenate | solution.py:136
  79.7 4.3 broadcast_in_dim.2
  84.0 93.7 %while.12 = (s32[]{:T(128)}, f32[2,2,512,1024]{3,2,1,0:T(8,128)}, s32[]{:T(128)}, s32[2]{0:T(128)S(1)}, s32[]{:T(128)}, /*index=5*/s32[2]{0:T(128)S(1)}, f32[4,2...) while((s32[]{:T(128)}, f32[2,2,512,1024]{3,2,1,0:T(8,128)}, ...), condition=%wide.region_6.7_spmd.clone.clone, body=%wide.region_0.6_spmd.clone.clone.sunk | while | flops 6523715584 | bytes 125305184 | solution.py:161
  89.0 1.7 dynamic-slice_bitcast_fusion.5
  92.2 1.3 fusion.631
  97.3 1.3 fusion.632
  98.5 1.3 fusion.635
  99.8 2.5 subtract_convert_fusion.7
  103.5 1.4 fusion.638
  108.7 1.3 fusion.639
  110.0 1.3 convolution_subtract_fusion.8
  111.2 1.5 subtract_convert_fusion.8
  114.0 1.3 fusion.644
  115.2 1.5 fusion.646
  116.7 1.3 fusion.647
  120.5 1.3 fusion.648
  121.7 1.3 add_reduce_fusion.3
  124.1 1.3 fusion.654
  125.3 1.3 fusion.655
  126.6 1.3 fusion.651
  127.9 1.3 fusion.652
  129.2 1.7 fusion.653
  130.9 1.3 convolution_add_fusion.7
  133.4 1.9 subtract_convert_fusion.9
  139.1 1.3 fusion.661
  141.6 1.3 fusion.659
  142.8 1.4 fusion.662
  144.3 2.4 add_convert_fusion.5
  150.5 1.3 fusion.668
  153.0 1.3 fusion.666
  154.2 1.3 convolution_subtract_fusion.9
  155.5 1.6 fusion.670
  157.2 1.8 maximum_add_fusion.2
  159.0 12.2 %dynamic_update_slice.6 = f32[2,2,512,1024]{3,2,1,0:T(8,128)} dynamic-update-slice(f32[2,2,512,1024]{3,2,1,0:T(8,128)} %get-tuple-element.510, f32[2,2,256,256]{3,2,1,0:T(8,128)S(1)} %maximum_add_fusion.2, s32[]{:T(128)} %constant.14.clone.1..sunk, s32[]{:T(128)} %constant.14.clone.1..sunk, s32[]{:T(128)S(6)} %select_n.300, s32[]{:T(128)S(6)} %select_n.301) | dynamic-update-slice | bytes 2097156 | tf_op jit(solution)/shard_map/while/body/dynamic_update_slice | solution.py:158
  177.8 5.5 %copy.109 = f32[256,8,8,128]{3,2,1,0:T(8,128)S(1)} copy(f32[256,8,8,128]{3,1,2,0:T(8,128)} %bitcast.455) | data formatting | bytes 16777216
  184.8 1.9 collective-permute-start.1
  187.6 44.6 %collective-permute-done.1 = f32[8192,128]{1,0:T(8,128)S(1)} collective-permute-done((f32[8192,128]{1,0:T(8,128)S(1)}, f32[8192,128]{1,0:T(8,128)S(1)}, u32[]{:S(2)}, u32[]{:S(2)}) %collective-permute-start.1) | collective-permute-done | bytes 4194336 | tf_op jit(solution)/shard_map/ppermute | solution.py:14
  232.2 2.4 bitcast_add_fusion
  234.6 194.3 %all-reduce.2.cloned.1.call-done = f32[8192,128]{1,0:T(8,128)} async-done(((f32[8192,128]{1,0:T(8,128)}), f32[8192,128]{1,0:T(8,128)}) %all-reduce.2.cloned.1.call-update) | async-done | bytes 4194320 | tf_op jit(solution)/shard_map/psum | solution.py:170
  428.9 6.0 %bitcast_subtract_fusion.1 = f32[8192,128]{1,0:T(8,128)} fusion(f32[16,2,2,128,128]{4,3,2,1,0:T(8,128)} %param.9, f32[8192,128]{1,0:T(8,128)} %all-reduce.2.cloned.1.call-done), kind=kLoop, calls=%fused_computation.379 | loop fusion | flops 2097152 | bytes 12582912 | tf_op jit(solution)/shard_map/sub | solution.py:171
  (38 shorter events, 30.9 us)
Async XLA Ops:
  6.5 422.4 %all-reduce.2.cloned.1.call-start = ((), (), s32[]{:S(2)}) async-start(), calls=%async_computation | async-start | bytes 8388608 | tf_op jit(solution)/shard_map/psum | solution.py:170
  6.5 53.4 %collective-permute-start = (f32[16,2,2,128,128]{4,3,2,1,0:T(8,128)}, f32[16,2,2,128,128]{4,3,2,1,0:T(8,128)}, u32[]{:S(2)}, u32[]{:S(2)}) collective-permute-start(f32[16,2,2,128,128]{4,3,2,1,0:T(8,128)} %param.9), channel_id=1, source_target_pairs={{8,0},{16,8},{24,16},{32,24},{40,32},{48,40},{56,48},{64,56},{72,6... | collective-permute-start | bytes 12582920 | tf_op jit(solution)/shard_map/ppermute | solution.py:14
  9.8 2.8 copy-start
  17.0 4.9 %copy-start.1 = (f32[256,256]{1,0:T(8,128)S(1)}, f32[256,256]{1,0:T(8,128)}, u32[]{:S(2)}) copy-start(f32[256,256]{1,0:T(8,128)} %param.11) | copy-start | bytes 786436
  79.7 4.3 copy-start.2
  79.7 4.3 copy-start.3
  184.8 47.4 %collective-permute-start.1 = (f32[8192,128]{1,0:T(8,128)S(1)}, f32[8192,128]{1,0:T(8,128)S(1)}, u32[]{:S(2)}, u32[]{:S(2)}) collective-permute-start(f32[8192,128]{1,0:T(8,128)S(1)} %bitcast.464), channel_id=1, source_target_pairs={{0,8},{8,16},{16,24},{24,32},{32,40},{40,48},{48,56},{56,64},{64,7... | collective-permute-start | bytes 12582920 | tf_op jit(solution)/shard_map/ppermute | solution.py:14
Sparse Core Ops, SparseCore 0:
  234.7 194.1 all-reduce.1
where the time goes:
time: 449 us; the launch traced here: 442 us
  waiting for transfers between devices  275 us (61%)
  matrix products  64.9 us (14%)
  local copies, waits for them, and re-layouts  52.4 us (12%)
  other arithmetic  19.9 us (4%)
  between operations  13.7 us (3%)
  loops' own time  10.6 us (2%)
  starting transfers between devices  5.2 us (1%)
    psum x1, waiting for transfers between devices, per_device(): combined = lax.psum(own_rows + arrived, 'pos')  194 us
    ppermute x2, waiting for transfers between devices, shifted(): return lax.ppermute(shard, axis, pairs)  81 us
    dot_general x24, matrix products, right_product(): jnp.einsum('mjk,kl->mjl', field, matrix, preferred_element_type=jnp.float32)  34.4 us
    dot_general x24, matrix products, left_product(): jnp.einsum('jk,mkl->mjl', matrix, field, preferred_element_type=jnp.float32)  30.5 us
    dynamic_update_slice x1, local copies, waits for them, and re-layouts, one_position(): return lax.dynamic_update_slice(gradient, former + term, corner)  12.2 us
    reshape x2, local copies, waits for them, and re-layouts, tiles_to_band(): tiles.reshape(band_tiles, across, slice_count, 2, tile_side, tile_side)  11 us
    another operation x1, loops' own time, per_device(): gradient = lax.fori_loop(0, live_count, one_position, empty)  10.6 us
    reshape x2, local copies, waits for them, and re-layouts, tiles_to_band(): shaped.reshape(slice_count, 2, band_tiles * tile_side, across * tile_side)  9.81 us
  transfers between devices with their start and end apart: 3, of which 3 were waited for; matrix products, arithmetic and copies ran while one was open for 3% of the time, Pallas kernels for 0%

commit v1 on v0

--- a/solution.py
+++ b/solution.py
@@ -120,6 +120,11 @@
 
 
 def per_device(object_tiles, probe, fresnel_phase, patterns, row_offsets, col_offsets, counts):
+
+    def process_the_trees(group_axis, buf):
+        small = jax.lax.all_gather(buf, group_axis).sum(axis=0)
+        return small
+
     slot_count = patterns.shape[2]
     pattern_side = patterns.shape[-1]
     tile_side = object_tiles.shape[-1]
@@ -167,7 +172,7 @@
     spill_rows = shaped[1]
     held_rows = object_tiles.reshape(-1, tile_side)
     arrived = shifted(spill_rows, "region", 1)
-    combined = lax.psum(own_rows + arrived, "pos")
+    combined = process_the_trees("pos", own_rows + arrived)
     return (held_rows - step_size * combined).reshape(object_tiles.shape)
 
 

time: 449 us -> 687 us (1.53)
  waiting for transfers between devices: 275 us -> 498 us
  other arithmetic: 19.9 us -> 33.4 us
    all_gather x0 -> x1, waiting for transfers between devices: none -> 417 us  [process_the_trees(): small = jax.lax.all_gather(buf, group_axis).sum(axis=0)]
    psum x1 -> x0, waiting for transfers between devices: 194 us -> none  [per_device(): combined = lax.psum(own_rows + arrived, 'pos')]
    reduce_sum x0 -> x1, other arithmetic: none -> 14 us  [process_the_trees(): small = jax.lax.all_gather(buf, group_axis).sum(axis=0)]
  transfers between devices with their start and end apart: 3 -> 3, of which waited for: 3 -> 3; matrix products, arithmetic and copies ran while one was open for 3% -> 2% of each run, Pallas kernels for 0% -> 0%
where the time goes in v1:
time: 687 us; the launch traced here: 679 us
  waiting for transfers between devices  498 us (72%)
  matrix products  64.9 us (9%)
  local copies, waits for them, and re-layouts  53.2 us (8%)
  other arithmetic  33.4 us (5%)
  between operations  13.7 us (2%)
  loops' own time  11.3 us (2%)
    all_gather x1, waiting for transfers between devices, process_the_trees(): small = jax.lax.all_gather(buf, group_axis).sum(axis=0)  417 us
    ppermute x2, waiting for transfers between devices, shifted(): return lax.ppermute(shard, axis, pairs)  80.9 us
    dot_general x24, matrix products, right_product(): jnp.einsum('mjk,kl->mjl', field, matrix, preferred_element_type=jnp.float32)  34.4 us
    dot_general x24, matrix products, left_product(): jnp.einsum('jk,mkl->mjl', matrix, field, preferred_element_type=jnp.float32)  30.5 us
    reduce_sum x1, other arithmetic, process_the_trees(): small = jax.lax.all_gather(buf, group_axis).sum(axis=0)  14 us
  transfers between devices with their start and end apart: 3, of which 3 were waited for; matrix products, arithmetic and copies ran while one was open for 2% of the time, Pallas kernels for 0%

profile of v1, /device:TPU:1, one launch (start us, length us, event | category | flops | bytes accessed | tf_op | source)
XLA Modules:
  0.0 679.5 jit_solution(8731446998546547487)
XLA Ops:
  6.5 3.3 collective-permute-start
  9.8 1.9 copy.160
  12.7 4.4 copy.215
  17.0 4.9 reshape.48
  22.0 1.6 fusion.370
  23.6 36.3 %collective-permute-done = f32[16,2,2,128,128]{4,3,2,1,0:T(8,128)} collective-permute-done((f32[16,2,2,128,128]{4,3,2,1,0:T(8,128)}, f32[16,2,2,128,128]{4,3,2,1,0:T(8,128)}, u32[]{:S(2)}, u32[]{:S(2)}) %collective-permute-start) | collective-permute-done | bytes 4194336 | tf_op jit(solution)/shard_map/ppermute | solution.py:14
  59.9 6.6 copy.214
  66.5 4.9 reshape.50
  71.4 8.3 %pad_maximum_fusion = f32[2,2,512,1024]{3,2,1,0:T(8,128)} fusion(f32[2,2,256,1024]{3,2,1,0:T(8,128)} %reshape.50, f32[2,2,256,1024]{3,2,1,0:T(8,128)} %reshape.48), kind=kLoop, calls=%fused_computation.377 | loop fusion | flops 2097152 | bytes 16777216 | tf_op jit(solution)/shard_map/concatenate | solution.py:141
  79.7 4.3 broadcast_in_dim.2
  84.0 94.6 %while.12 = (s32[]{:T(128)}, f32[2,2,512,1024]{3,2,1,0:T(8,128)}, s32[]{:T(128)}, s32[2]{0:T(128)S(1)}, s32[]{:T(128)}, /*index=5*/s32[2]{0:T(128)S(1)}, f32[4,2...) while((s32[]{:T(128)}, f32[2,2,512,1024]{3,2,1,0:T(8,128)}, ...), condition=%wide.region_6.7_spmd.clone.clone, body=%wide.region_0.6_spmd.clone.clone.sunk | while | flops 6523715584 | bytes 125305184 | solution.py:166
  89.0 1.7 dynamic-slice_bitcast_fusion.5
  94.7 1.3 fusion.634
  97.3 1.3 fusion.632
  98.5 1.3 fusion.635
  99.8 2.5 subtract_convert_fusion.7
  103.5 1.4 fusion.638
  106.2 1.3 fusion.641
  110.0 1.3 convolution_subtract_fusion.8
  111.3 1.5 subtract_convert_fusion.8
  114.0 1.3 fusion.644
  115.3 1.5 fusion.646
  119.2 1.3 fusion.645
  120.5 1.3 fusion.648
  121.8 1.3 add_reduce_fusion.3
  124.1 1.3 fusion.654
  125.4 1.3 fusion.655
  126.7 1.3 fusion.651
  127.9 1.3 fusion.652
  129.2 1.7 fusion.653
  130.9 1.3 convolution_add_fusion.7
  133.4 1.9 subtract_convert_fusion.9
  139.1 1.3 fusion.661
  142.9 1.4 fusion.662
  144.3 2.4 add_convert_fusion.5
  150.5 1.3 fusion.668
  154.3 1.3 convolution_subtract_fusion.9
  155.5 1.6 fusion.670
  157.2 1.8 maximum_add_fusion.2
  159.1 12.2 %dynamic_update_slice.6 = f32[2,2,512,1024]{3,2,1,0:T(8,128)} dynamic-update-slice(f32[2,2,512,1024]{3,2,1,0:T(8,128)} %get-tuple-element.532, f32[2,2,256,256]{3,2,1,0:T(8,128)S(1)} %maximum_add_fusion.2, s32[]{:T(128)} %constant.10.clone.1..sunk, s32[]{:T(128)} %constant.10.clone.1..sunk, s32[]{:T(128)S(6)} %select_n.300, s32[]{:T(128)S(6)} %select_n.301) | dynamic-update-slice | bytes 2097156 | tf_op jit(solution)/shard_map/while/body/dynamic_update_slice | solution.py:163
  178.6 5.5 copy.211
  185.6 1.9 collective-permute-start.1
  188.4 44.6 %collective-permute-done.1 = f32[8192,128]{1,0:T(8,128)S(1)} collective-permute-done((f32[8192,128]{1,0:T(8,128)S(1)}, f32[8192,128]{1,0:T(8,128)S(1)}, u32[]{:S(2)}, u32[]{:S(2)}) %collective-permute-start.1) | collective-permute-done | bytes 4194336 | tf_op jit(solution)/shard_map/ppermute | solution.py:14
  233.0 2.4 bitcast_add_fusion
  235.4 416.7 %all-gather.3.cloned.1.call-done = f32[65536,128]{1,0:T(8,128)} async-done(((f32[8192,128]{1,0:T(8,128)}), f32[65536,128]{1,0:T(8,128)}) %all-gather.3.cloned.1.call-update) | async-done | bytes 33554448 | tf_op jit(solution)/shard_map/all_gather | solution.py:125
  652.2 14.0 %reduce_sum.56 = f32[8192,128]{1,0:T(8,128)} reduce(f32[8,8192,128]{2,1,0:T(8,128)} %bitcast.455, f32[]{:T(128)} %constant.11.clone.1), dimensions={0}, to_apply=%region_7.8 | reduce | flops 7340032 | bytes 37748740 | tf_op jit(solution)/shard_map/reduce_sum | solution.py:125
  666.2 2.7 broadcast_multiply_fusion
  669.6 2.8 sub.74
  (42 shorter events, 34.1 us)
Async XLA Ops:
  6.5 645.6 %all-gather.3.cloned.1.call-start = ((), (), s32[]{:S(2)}) async-start(), calls=%async_computation | async-start | bytes 37748736 | tf_op jit(solution)/shard_map/all_gather | solution.py:125
  6.5 53.4 %collective-permute-start = (f32[16,2,2,128,128]{4,3,2,1,0:T(8,128)}, f32[16,2,2,128,128]{4,3,2,1,0:T(8,128)}, u32[]{:S(2)}, u32[]{:S(2)}) collective-permute-start(f32[16,2,2,128,128]{4,3,2,1,0:T(8,128)} %param.9), channel_id=1, source_target_pairs={{8,0},{16,8},{24,16},{32,24},{40,32},{48,40},{56,48},{64,56},{72,6... | collective-permute-start | bytes 12582920 | tf_op jit(solution)/shard_map/ppermute | solution.py:14
  9.8 2.8 copy-start
  17.0 4.9 copy-start.2
  79.7 4.3 copy-start.3
  79.7 4.3 copy-start.4
  185.6 47.4 %collective-permute-start.1 = (f32[8192,128]{1,0:T(8,128)S(1)}, f32[8192,128]{1,0:T(8,128)S(1)}, u32[]{:S(2)}, u32[]{:S(2)}) collective-permute-start(f32[8192,128]{1,0:T(8,128)S(1)} %bitcast.465), channel_id=1, source_target_pairs={{0,8},{8,16},{16,24},{24,32},{32,40},{40,48},{48,56},{56,64},{64,7... | collective-permute-start | bytes 12582920 | tf_op jit(solution)/shard_map/ppermute | solution.py:14
  666.2 3.4 copy-start.1
Sparse Core Ops, SparseCore 0:
  235.6 416.5 all-gather.2
